TPU v7x, 128 devices: a whole 4x4x4 slice. The times are simulated.
128 devices in a mesh: gx: 8 (over x, core), gy: 16 (over z, y).
Axes of the slice: x: 4, y: 4, z: 4, core: 2. Of those that a mesh axis runs over, the one named last changes fastest.
Arguments:
- multipole: bfloat16 [65536, 256], P(('gx', 'gy')), may hold values from -6 to 6
- coarse_local: bfloat16 [256, 256], P('gx'), may hold values from -6 to 6
- send_rows: int32 [128, 128, 16], P(('gx', 'gy')), may hold values from 0 to 511
- list_src: int32 [65536, 64], P(('gx', 'gy')), may hold values from 0 to 2559
- list_vec: int32 [65536, 64], P(('gx', 'gy')), may hold values from 0 to 15
- list_len: int32 [65536], P(('gx', 'gy')), may hold values from 16 to 64, as said below
- parent_of: int32 [65536], P(('gx', 'gy')), may hold values from 0 to 255
- octant: int32 [65536], P(('gx', 'gy')), may hold values from 0 to 7
- m2l_ops: bfloat16 [16, 256, 256], replicated, may hold values from -0.0625 to 0.0625
- l2l_ops: bfloat16 [8, 256, 256], replicated, may hold values from -0.375 to 0.375
- near_list: int32 [65536, 8], P(('gx', 'gy')), may hold values from 0 to 575, as said below
- positions: float32 [3, 2097152], P(None, ('gx', 'gy')), may hold values from 0 to 1
- charges: float32 [2097152], P(('gx', 'gy')), may hold values from -0.75 to 0.75
- basis: bfloat16 [2097152, 256], P(('gx', 'gy')), may hold values from -0.375 to 0.375
Outputs:
- leaf_local: float32 [65536, 256], P(('gx', 'gy'))
- potential: float32 [2097152], P(('gx', 'gy'))
Inputs may be any that keep to these rules, and one draw needn't show every extreme that they name: `list_len`: the first cell of every device uses all 64 slots. `near_list`: cell i of a device lists extended cells i to i + 64.
All inputs are finite; a program needn't handle non-finite values.
Results may differ from a plain program's by a relative error of at most 0.0024.
Values may be sent and summed in bfloat16 or wider, within the bound.
A program may use at most 64 MiB of HBM per device.

v0:
```python
import jax
import jax.numpy as jnp
from jax import lax
from jax.sharding import PartitionSpec as P

PART = 32
RIM = 32


softening = 0.01


def shifted_2(shard, axis, by):
    peers = lax.axis_size(axis)
    pairs = [(i, i + by) for i in range(peers) if 0 <= i + by < peers]
    return lax.ppermute(shard, axis, pairs)


def near_sum(targets, tiles):
    total = jnp.zeros((targets.shape[1], targets.shape[2], tiles.shape[2]), jnp.float32)
    for axis_index in range(3):
        gap = targets[axis_index][:, :, None] - tiles[axis_index][:, None, :]
        total = total + gap * gap
    return jnp.sum(tiles[3][:, None, :] * lax.rsqrt(total + softening), axis=2)


def shards(
    multipole,
    coarse_local,
    send_rows,
    list_src,
    list_vec,
    list_len,
    parent_of,
    octant,
    m2l_ops,
    l2l_ops,
    near_list,
    positions,
    charges,
    basis,
):
    cells = multipole.shape[0]
    width = multipole.shape[1]
    slots = send_rows.shape[2]
    list_block = min(cells, 128)
    list_blocks = cells // list_block
    near_block_size = min(cells, 128)
    near_blocks = cells // near_block_size
    outgoing = multipole[send_rows[0].reshape(-1)].reshape(-1, slots, width)
    incoming = lax.all_to_all(outgoing, ("gx", "gy"), split_axis=0, concat_axis=0, tiled=True)
    table = jnp.concatenate([multipole, incoming.reshape(-1, width)], axis=0)
    classes = jnp.arange(m2l_ops.shape[0], dtype=jnp.int32)
    slot_iota = jnp.arange(list_src.shape[1], dtype=jnp.int32)

    def translate(items):
        src, vec, lengths = items
        select = (
            (vec[:, :, None] == classes[None, None, :])
            & (slot_iota[None, :, None] < lengths[:, None, None])
        ).astype(jnp.bfloat16)
        rows = table[src]
        grouped = jnp.einsum(
            "bkv,bkp->bvp", select, rows, preferred_element_type=jnp.float32
        ).astype(jnp.bfloat16)
        return jnp.einsum("bvp,vpq->bq", grouped, m2l_ops, preferred_element_type=jnp.float32)

    far = lax.map(
        translate,
        (
            list_src.reshape(list_blocks, list_block, -1),
            list_vec.reshape(list_blocks, list_block, -1),
            list_len.reshape(list_blocks, list_block),
        ),
    )
    far = far.reshape(cells, width)
    whole = lax.all_gather(coarse_local, "gx", axis=0, tiled=True)
    shifted = jnp.einsum("cp,opq->coq", whole, l2l_ops, preferred_element_type=jnp.float32)
    flat_shifted = shifted.reshape(-1, width)
    down = flat_shifted[parent_of * 8 + octant]
    leaf_local = far + down
    rounded = leaf_local.astype(jnp.bfloat16)
    farpot = jnp.einsum(
        "cjp,cp->cj", basis.reshape(cells, PART, width), rounded, preferred_element_type=jnp.float32
    ).reshape(-1)
    data = jnp.concatenate([positions, charges[None, :]], axis=0)
    lower = shifted_2(data[:, (cells - RIM) * PART :], ("gx", "gy"), 1)
    upper = shifted_2(data[:, : RIM * PART], ("gx", "gy"), -1)
    extended = jnp.concatenate([lower, data, upper], axis=1).reshape(4, cells + 2 * RIM, PART)
    targets = positions.reshape(3, near_blocks, near_block_size, PART).transpose(1, 0, 2, 3)

    def near_block(items):
        neighbors, target_block = items
        tiles = extended[:, neighbors].reshape(4, neighbors.shape[0], -1)
        return near_sum(target_block, tiles)

    nearpot = lax.map(
        near_block, (near_list.reshape(near_blocks, near_block_size, -1), targets)
    ).reshape(-1)
    return (leaf_local, farpot + nearpot)


def solution(mesh):
    placed = (
        P(("gx", "gy"), None),
        P("gx", None),
        P(("gx", "gy"), None, None),
        P(("gx", "gy"), None),
        P(("gx", "gy"), None),
        P(("gx", "gy")),
        P(("gx", "gy")),
        P(("gx", "gy")),
        P(),
        P(),
        P(("gx", "gy"), None),
        P(None, ("gx", "gy")),
        P(("gx", "gy")),
        P(("gx", "gy"), None),
    )
    return jax.shard_map(
        shards,
        mesh=mesh,
        in_specs=placed,
        out_specs=(P(("gx", "gy"), None), P(("gx", "gy"))),
        check_vma=False,
    )
```

profile of v0, /device:TPU:1, one launch (start us, length us, event | category | flops | bytes accessed | tf_op | source)
XLA Modules:
  0.0 297.0 jit_solution(1609399353656894980)
XLA Ops:
  1.5 4.0 %collective-permute-start = (f32[4,1024]{1,0:T(4,128)S(1)}, f32[4,1024]{1,0:T(4,128)S(1)}, u32[]{:S(2)}, u32[]{:S(2)}) collective-permute-start(f32[4,1024]{1,0:T(4,128)S(1)} %get-tuple-element.150), channel_id=1, source_target_pairs={{0,1},{1,2},{2,3},{3,4},{4,5},{5,6},{6,7},{7,8},{8,9},{9,10},{10,1... | collective-permute-start | bytes 49160 | tf_op jit(solution)/shard_map/ppermute | solution.py:16
  5.6 7.4 %collective-permute-start.1 = (f32[4,1024]{1,0:T(4,128)S(1)}, f32[4,1024]{1,0:T(4,128)S(1)}, u32[]{:S(2)}, u32[]{:S(2)}) collective-permute-start(f32[4,1024]{1,0:T(4,128)S(1)} %get-tuple-element.151), channel_id=1, source_target_pairs={{1,0},{2,1},{3,2},{4,3},{5,4},{6,5},{7,6},{8,7},{9,8},{10,9},{11,1... | collective-permute-start | bytes 49160 | tf_op jit(solution)/shard_map/ppermute | solution.py:16
  14.0 9.0 %gather_fusion.2 = bf16[2048,256]{1,0:T(8,128)(2,1)} fusion(bf16[512,256]{1,0:T(8,128)(2,1)S(1)} %copy-done.1, s32[2048]{0:T(1024)S(1)} %broadcast_clamp_fusion.2), kind=kCustom, calls=%fused_computation.2 | custom fusion | bytes 2105344 | tf_op jit(solution)/shard_map/gather | solution.py:50
  22.9 6.4 %all-to-all-start = ((bf16[128,16,256]{2,1,0:T(8,128)(2,1)}), bf16[128,16,256]{2,1,0:T(8,128)(2,1)}, u32[]{:S(2)}, u32[]{:S(2)}) async-start(bf16[128,16,256]{2,1,0:T(8,128)(2,1)} %bitcast.14), calls=%async_computation | async-start | bytes 2097152 | tf_op jit(solution)/shard_map/all_to_all | solution.py:51
  29.3 21.3 %all_gather.3 = bf16[256,256]{1,0:T(8,128)(2,1)S(1)} all-gather(bf16[32,256]{1,0:T(8,128)(2,1)S(1)} %copy-done.8), channel_id=1, replica_groups=mesh['gx'=8,'gy'=16] {'gx'}, dimensions={0}, use_global_device_ids=true | all-gather | bytes 147456 | tf_op jit(solution)/shard_map/all_gather | solution.py:77
  50.7 1.8 fusion.10
  52.5 1.2 reshape.199
  56.0 2.8 copy.66
  58.9 2.2 gather_fusion.3
  61.1 1.1 pad_maximum_fusion.1
  62.6 1.8 copy.55
  64.4 58.8 %while.21 = (s32[]{:T(128)}, f32[4,128,32]{2,1,0:T(8,128)}, s32[4,128,8]{2,1,0:T(8,128)}, f32[4,576,32]{2,0,1:T(4,128)}, f32[4,3,128,32]{3,2,0,1:T(8,128)}, /*index=5*/s32[]{:T(128)}) while((s32[]{:T(128)}, f32[4,128,32]{2,1,0:T(8,128)}, s32[4,128,8]{2,1,0:T(8,128)}, f32[4,576,32]{2,0,1:T(4,128)}, f32[4,3,128,32]{3,2,0,1:T(8,128)}, ...), condition=%wide.region_4.5_spmd, body=%wide.region_2.4_spmd.sunk | while | flops 11534338 | bytes 5091417 | solution.py:97
  65.4 1.0 dynamic-slice_bitcast_fusion.2
  67.0 4.8 %gather_fusion = f32[1024,4,32]{2,1,0:T(4,128)S(1)} fusion(f32[4,576,32]{2,0,1:T(4,128)} %get-tuple-element.279, s32[1024]{0:T(1024)S(1)} %broadcast_clamp_fusion.5), kind=kCustom, calls=%fused_computation.1.clone.1 | custom fusion | bytes 1052672 | tf_op jit(solution)/shard_map/while/body/eval_jaxpr/gather | solution.py:94
  71.8 1.6 copy.74
  73.4 1.1 fusion.26
  75.0 3.5 %multiply_reduce_fusion.2 = f32[128,32]{1,0:T(8,128)S(1)} fusion(f32[128,256]{1,0:T(8,128)S(1)} %copy.75, f32[128,32]{1,0:T(8,128)S(1)} %get-tuple-element.227, f32[128,256]{1,0:T(8,128)S(1)} %copy.76, f32[128,32]{1,0:T(8,128)} %get-tuple-element.229, f32[128,256]{1,0:T(8,128)S(1)} %copy.77, f32[128,32]{1,0:T(8,128)S(1)} %get-tuple-element.231, ...), kind=kLoop, calls=%fused_computation.6.clone.1 | loop fusion | flops 11530240 | bytes 589824 | tf_op jit(solution)/shard_map/while/body/eval_jaxpr/reduce_sum | solution.py:24
  81.7 4.8 %gather_fusion = f32[1024,4,32]{2,1,0:T(4,128)S(1)} fusion(f32[4,576,32]{2,0,1:T(4,128)} %get-tuple-element.279, s32[1024]{0:T(1024)S(1)} %broadcast_clamp_fusion.5), kind=kCustom, calls=%fused_computation.1.clone.1 | custom fusion | bytes 1052672 | tf_op jit(solution)/shard_map/while/body/eval_jaxpr/gather | solution.py:94
  86.5 1.6 copy.74
  88.1 1.1 fusion.26
  89.7 3.5 %multiply_reduce_fusion.2 = f32[128,32]{1,0:T(8,128)S(1)} fusion(f32[128,256]{1,0:T(8,128)S(1)} %copy.75, f32[128,32]{1,0:T(8,128)S(1)} %get-tuple-element.227, f32[128,256]{1,0:T(8,128)S(1)} %copy.76, f32[128,32]{1,0:T(8,128)} %get-tuple-element.229, f32[128,256]{1,0:T(8,128)S(1)} %copy.77, f32[128,32]{1,0:T(8,128)S(1)} %get-tuple-element.231, ...), kind=kLoop, calls=%fused_computation.6.clone.1 | loop fusion | flops 11530240 | bytes 589824 | tf_op jit(solution)/shard_map/while/body/eval_jaxpr/reduce_sum | solution.py:24
  94.8 1.0 dynamic-slice_bitcast_fusion.2
  96.4 4.8 %gather_fusion = f32[1024,4,32]{2,1,0:T(4,128)S(1)} fusion(f32[4,576,32]{2,0,1:T(4,128)} %get-tuple-element.279, s32[1024]{0:T(1024)S(1)} %broadcast_clamp_fusion.5), kind=kCustom, calls=%fused_computation.1.clone.1 | custom fusion | bytes 1052672 | tf_op jit(solution)/shard_map/while/body/eval_jaxpr/gather | solution.py:94
  101.2 1.6 copy.74
  102.8 1.1 fusion.26
  104.4 3.5 %multiply_reduce_fusion.2 = f32[128,32]{1,0:T(8,128)S(1)} fusion(f32[128,256]{1,0:T(8,128)S(1)} %copy.75, f32[128,32]{1,0:T(8,128)S(1)} %get-tuple-element.227, f32[128,256]{1,0:T(8,128)S(1)} %copy.76, f32[128,32]{1,0:T(8,128)} %get-tuple-element.229, f32[128,256]{1,0:T(8,128)S(1)} %copy.77, f32[128,32]{1,0:T(8,128)S(1)} %get-tuple-element.231, ...), kind=kLoop, calls=%fused_computation.6.clone.1 | loop fusion | flops 11530240 | bytes 589824 | tf_op jit(solution)/shard_map/while/body/eval_jaxpr/reduce_sum | solution.py:24
  109.5 1.0 dynamic-slice_bitcast_fusion.2
  111.1 4.8 %gather_fusion = f32[1024,4,32]{2,1,0:T(4,128)S(1)} fusion(f32[4,576,32]{2,0,1:T(4,128)} %get-tuple-element.279, s32[1024]{0:T(1024)S(1)} %broadcast_clamp_fusion.5), kind=kCustom, calls=%fused_computation.1.clone.1 | custom fusion | bytes 1052672 | tf_op jit(solution)/shard_map/while/body/eval_jaxpr/gather | solution.py:94
  115.9 1.6 copy.74
  117.5 1.1 fusion.26
  119.1 3.5 %multiply_reduce_fusion.2 = f32[128,32]{1,0:T(8,128)S(1)} fusion(f32[128,256]{1,0:T(8,128)S(1)} %copy.75, f32[128,32]{1,0:T(8,128)S(1)} %get-tuple-element.227, f32[128,256]{1,0:T(8,128)S(1)} %copy.76, f32[128,32]{1,0:T(8,128)} %get-tuple-element.229, f32[128,256]{1,0:T(8,128)S(1)} %copy.77, f32[128,32]{1,0:T(8,128)S(1)} %get-tuple-element.231, ...), kind=kLoop, calls=%fused_computation.6.clone.1 | loop fusion | flops 11530240 | bytes 589824 | tf_op jit(solution)/shard_map/while/body/eval_jaxpr/reduce_sum | solution.py:24
  123.2 1.1 reshape.200
  124.3 1.3 pad_maximum_fusion
  125.6 163.0 %while.22 = (s32[]{:T(128)}, f32[4,128,256]{2,1,0:T(8,128)}, s32[4,128,64]{1,0,2:T(4,128)}, s32[4,128]{1,0:T(4,128)}, s32[4,128,64]{2,1,0:T(8,128)}, /*index=5*/...) while((s32[]{:T(128)}, f32[4,128,256]{2,1,0:T(8,128)}, ...), condition=%wide.region_1.2_spmd.clone, body=%wide.region_0.1_spmd.clone.sunk | while | flops 336371712 | bytes 26166920 | solution.py:68
  129.1 32.9 %gather_fusion.1 = bf16[8192,256]{1,0:T(8,128)(2,1)} fusion(bf16[2560,256]{1,0:T(8,128)(2,1)S(1)} %get-tuple-element.261, s32[8192]{0:T(1024)S(1)} %broadcast_clamp_fusion.6), kind=kCustom, calls=%fused_computation.clone.clone.1 | custom fusion | bytes 8421376 | tf_op jit(solution)/shard_map/while/body/eval_jaxpr/gather | solution.py:62
  162.0 3.0 %convolution_convert_fusion.2 = bf16[128,16,256]{2,1,0:T(8,128)(2,1)S(1)} fusion(pred[128,64,16]{1,2,0:T(8,128)(4,1)S(1)} %copy.80, bf16[128,64,256]{2,1,0:T(8,128)(2,1)} %bitcast.100), kind=kOutput, calls=%fused_computation.14.clone.1 | convolution fusion | flops 67633152 | bytes 5373952 | tf_op jit(solution)/shard_map/while/body/eval_jaxpr/bkv,bkp->bvp/dot_general | solution.py:63
  165.0 1.4 fusion.33
  169.8 32.9 %gather_fusion.1 = bf16[8192,256]{1,0:T(8,128)(2,1)} fusion(bf16[2560,256]{1,0:T(8,128)(2,1)S(1)} %get-tuple-element.261, s32[8192]{0:T(1024)S(1)} %broadcast_clamp_fusion.6), kind=kCustom, calls=%fused_computation.clone.clone.1 | custom fusion | bytes 8421376 | tf_op jit(solution)/shard_map/while/body/eval_jaxpr/gather | solution.py:62
  202.7 3.0 %convolution_convert_fusion.2 = bf16[128,16,256]{2,1,0:T(8,128)(2,1)S(1)} fusion(pred[128,64,16]{1,2,0:T(8,128)(4,1)S(1)} %copy.80, bf16[128,64,256]{2,1,0:T(8,128)(2,1)} %bitcast.100), kind=kOutput, calls=%fused_computation.14.clone.1 | convolution fusion | flops 67633152 | bytes 5373952 | tf_op jit(solution)/shard_map/while/body/eval_jaxpr/bkv,bkp->bvp/dot_general | solution.py:63
  205.7 1.4 fusion.33
  210.6 32.9 %gather_fusion.1 = bf16[8192,256]{1,0:T(8,128)(2,1)} fusion(bf16[2560,256]{1,0:T(8,128)(2,1)S(1)} %get-tuple-element.261, s32[8192]{0:T(1024)S(1)} %broadcast_clamp_fusion.6), kind=kCustom, calls=%fused_computation.clone.clone.1 | custom fusion | bytes 8421376 | tf_op jit(solution)/shard_map/while/body/eval_jaxpr/gather | solution.py:62
  243.5 3.0 %convolution_convert_fusion.2 = bf16[128,16,256]{2,1,0:T(8,128)(2,1)S(1)} fusion(pred[128,64,16]{1,2,0:T(8,128)(4,1)S(1)} %copy.80, bf16[128,64,256]{2,1,0:T(8,128)(2,1)} %bitcast.100), kind=kOutput, calls=%fused_computation.14.clone.1 | convolution fusion | flops 67633152 | bytes 5373952 | tf_op jit(solution)/shard_map/while/body/eval_jaxpr/bkv,bkp->bvp/dot_general | solution.py:63
  246.5 1.4 fusion.33
  251.3 32.9 %gather_fusion.1 = bf16[8192,256]{1,0:T(8,128)(2,1)} fusion(bf16[2560,256]{1,0:T(8,128)(2,1)S(1)} %get-tuple-element.261, s32[8192]{0:T(1024)S(1)} %broadcast_clamp_fusion.6), kind=kCustom, calls=%fused_computation.clone.clone.1 | custom fusion | bytes 8421376 | tf_op jit(solution)/shard_map/while/body/eval_jaxpr/gather | solution.py:62
  284.2 3.0 %convolution_convert_fusion.2 = bf16[128,16,256]{2,1,0:T(8,128)(2,1)S(1)} fusion(pred[128,64,16]{1,2,0:T(8,128)(4,1)S(1)} %copy.80, bf16[128,64,256]{2,1,0:T(8,128)(2,1)} %bitcast.100), kind=kOutput, calls=%fused_computation.14.clone.1 | convolution fusion | flops 67633152 | bytes 5373952 | tf_op jit(solution)/shard_map/while/body/eval_jaxpr/bkv,bkp->bvp/dot_general | solution.py:63
  287.2 1.4 fusion.33
  288.7 1.9 convert_bitcast_fusion
  290.6 5.6 %fusion.8 = f32[512,1,32]{2,1,0:T(1,128)S(1)} fusion(bf16[512,32,256]{2,1,0:T(8,128)(2,1)} %bitcast.116, bf16[512,256,1]{1,0,2:T(8,128)(2,1)S(1)} %get-tuple-element.141), kind=kOutput, calls=%fused_computation.29 | convolution fusion | flops 8388608 | bytes 8716288 | tf_op jit(solution)/shard_map/cjp,cp->cj/dot_general | solution.py:83
  (117 shorter events, 30.4 us)
Async XLA Ops:
  0.6 50.0 %copy-start = (bf16[8,256,256]{2,1,0:T(8,128)(2,1)S(1)}, bf16[8,256,256]{2,1,0:T(8,128)(2,1)}, u32[]{:S(2)}) copy-start(bf16[8,256,256]{2,1,0:T(8,128)(2,1)} %param.27) | copy-start | bytes 3145732
  0.6 13.3 %copy-start.1 = (bf16[512,256]{1,0:T(8,128)(2,1)S(1)}, bf16[512,256]{1,0:T(8,128)(2,1)}, u32[]{:S(2)}) copy-start(bf16[512,256]{1,0:T(8,128)(2,1)} %param.18) | copy-start | bytes 786436
  1.5 59.6 %collective-permute-start = (f32[4,1024]{1,0:T(4,128)S(1)}, f32[4,1024]{1,0:T(4,128)S(1)}, u32[]{:S(2)}, u32[]{:S(2)}) collective-permute-start(f32[4,1024]{1,0:T(4,128)S(1)} %get-tuple-element.150), channel_id=1, source_target_pairs={{0,1},{1,2},{2,3},{3,4},{4,5},{5,6},{6,7},{7,8},{8,9},{9,10},{10,1... | collective-permute-start | bytes 49160 | tf_op jit(solution)/shard_map/ppermute | solution.py:16
  5.6 55.5 %collective-permute-start.1 = (f32[4,1024]{1,0:T(4,128)S(1)}, f32[4,1024]{1,0:T(4,128)S(1)}, u32[]{:S(2)}, u32[]{:S(2)}) collective-permute-start(f32[4,1024]{1,0:T(4,128)S(1)} %get-tuple-element.151), channel_id=1, source_target_pairs={{1,0},{2,1},{3,2},{4,3},{5,4},{6,5},{7,6},{8,7},{9,8},{10,9},{11,1... | collective-permute-start | bytes 49160 | tf_op jit(solution)/shard_map/ppermute | solution.py:16
  13.9 15.4 %copy-start.8 = (bf16[32,256]{1,0:T(8,128)(2,1)S(1)}, bf16[32,256]{1,0:T(8,128)(2,1)}, u32[]{:S(2)}) copy-start(bf16[32,256]{1,0:T(8,128)(2,1)} %param.19) | copy-start | bytes 49156
  13.9 36.7 %copy-start.10 = (s32[512]{0:T(512)S(1)}, s32[512]{0:T(512)}, u32[]{:S(2)}) copy-start(s32[512]{0:T(512)} %param.25) | copy-start | bytes 6148
  13.9 36.7 %copy-start.11 = (s32[512]{0:T(512)S(1)}, s32[512]{0:T(512)}, u32[]{:S(2)}) copy-start(s32[512]{0:T(512)} %param.24) | copy-start | bytes 6148
  22.9 29.5 %copy-start.3 = (f32[3,16384]{1,0:T(4,128)S(1)}, f32[3,16384]{1,0:T(4,128)}, u32[]{:S(2)}) copy-start(f32[3,16384]{1,0:T(4,128)} %param.29) | copy-start | bytes 589828
  22.9 30.7 %copy-start.7 = (s32[512,64]{0,1:T(8,128)S(1)}, s32[512,64]{0,1:T(8,128)}, u32[]{:S(2)}) copy-start(s32[512,64]{0,1:T(8,128)} %param.22) | copy-start | bytes 393220
  22.9 31.4 %copy-start.6 = (s32[512,64]{0,1:T(8,128)S(1)}, s32[512,64]{0,1:T(8,128)}, u32[]{:S(2)}) copy-start(s32[512,64]{0,1:T(8,128)} %param.21) | copy-start | bytes 393220
  22.9 32.3 %copy-start.9 = (s32[512,8]{0,1:T(8,128)S(1)}, s32[512,8]{0,1:T(8,128)}, u32[]{:S(2)}) copy-start(s32[512,8]{0,1:T(8,128)} %param.28) | copy-start | bytes 49156
  22.9 101.3 %all-to-all-start = ((bf16[128,16,256]{2,1,0:T(8,128)(2,1)}), bf16[128,16,256]{2,1,0:T(8,128)(2,1)}, u32[]{:S(2)}, u32[]{:S(2)}) async-start(bf16[128,16,256]{2,1,0:T(8,128)(2,1)} %bitcast.14), calls=%async_computation | async-start | bytes 2097152 | tf_op jit(solution)/shard_map/all_to_all | solution.py:51
  56.0 5.1 %copy-start.5 = (f32[16384]{0:T(1024)S(1)}, f32[16384]{0:T(1024)}, u32[]{:S(2)}) copy-start(f32[16384]{0:T(1024)} %param.30) | copy-start | bytes 196612
  125.6 163.1 %copy-start.4 = (f32[512,256]{1,0:T(8,128)S(1)}, f32[512,256]{1,0:T(8,128)}, u32[]{:S(2)}) copy-start(f32[512,256]{1,0:T(8,128)} %gather_fusion.3) | copy-start | bytes 1572868
  162.0 3.0 %copy-start.2 = (bf16[16,256,256]{2,1,0:T(8,128)(2,1)S(1)}, bf16[16,256,256]{2,1,0:T(8,128)(2,1)}, u32[]{:S(2)}) copy-start(bf16[16,256,256]{2,1,0:T(8,128)(2,1)} %get-tuple-element.262) | copy-start | bytes 6291460 | tf_op jit(solution)/shard_map/while
  202.7 3.0 %copy-start.2 = (bf16[16,256,256]{2,1,0:T(8,128)(2,1)S(1)}, bf16[16,256,256]{2,1,0:T(8,128)(2,1)}, u32[]{:S(2)}) copy-start(bf16[16,256,256]{2,1,0:T(8,128)(2,1)} %get-tuple-element.262) | copy-start | bytes 6291460 | tf_op jit(solution)/shard_map/while
  243.5 3.0 %copy-start.2 = (bf16[16,256,256]{2,1,0:T(8,128)(2,1)S(1)}, bf16[16,256,256]{2,1,0:T(8,128)(2,1)}, u32[]{:S(2)}) copy-start(bf16[16,256,256]{2,1,0:T(8,128)(2,1)} %get-tuple-element.262) | copy-start | bytes 6291460 | tf_op jit(solution)/shard_map/while
  284.2 3.0 %copy-start.2 = (bf16[16,256,256]{2,1,0:T(8,128)(2,1)S(1)}, bf16[16,256,256]{2,1,0:T(8,128)(2,1)}, u32[]{:S(2)}) copy-start(bf16[16,256,256]{2,1,0:T(8,128)(2,1)} %get-tuple-element.262) | copy-start | bytes 6291460 | tf_op jit(solution)/shard_map/while
where the time goes:
time: 299 us; the launch traced here: 297 us
  local copies, waits for them, and re-layouts  204 us (68%)
  other arithmetic  27.3 us (9%)
  matrix products  25.1 us (8%)
  blocking collectives  21.3 us (7%)
  starting transfers between devices  17.8 us (6%)
    gather x4, local copies, waits for them, and re-layouts, translate(): rows = table[src]  132 us
    gather x8, local copies, waits for them, and re-layouts, near_block(): tiles = extended[:, neighbors].reshape(4, neighbors.shape[0], -1)  25.7 us
    all_gather x1, blocking collectives, shards(): whole = lax.all_gather(coarse_local, 'gx', axis=0, tiled=True)  21.3 us
    reduce_sum x4, other arithmetic, near_sum(): return jnp.sum(tiles[3][:, None, :] * lax.rsqrt(total + softening), axis=2)  14.1 us
    dot_general x4, matrix products, translate(): jnp.einsum('bkv,bkp->bvp', select, rows, preferred_element_type=jnp.float32)  11.9 us
    ppermute x2, starting transfers between devices, shifted_2(): return lax.ppermute(shard, axis, pairs)  11.4 us
    gather x1, local copies, waits for them, and re-layouts, shards(): outgoing = multipole[send_rows[0].reshape(-1)].reshape(-1, slots, width)  8.98 us
    all_to_all x1, starting transfers between devices, shards(): lax.all_to_all(outgoing, ('gx', 'gy'), split_axis=0, concat_axis=0, tiled...  6.38 us
  transfers between devices with their start and end apart: 3, of which 0 were waited for; matrix products, arithmetic and copies ran while one was open for 28% of the time, Pallas kernels for 0%

commit v1 on v0

v1 whole, which is shorter than its diff:
```python
import functools

import jax
import jax.numpy as jnp
from jax import lax
from jax.experimental import pallas as pl
from jax.experimental.pallas import tpu as pltpu
from jax.sharding import PartitionSpec as P

BF = jnp.bfloat16
F8 = jnp.float8_e4m3fn
F32 = jnp.float32
I32 = jnp.int32
SOFT = 0.01


def iota(shape, axis):
    return lax.broadcasted_iota(I32, shape, axis)


def dot(a, b):
    return jnp.dot(a, b, preferred_element_type=F32)


def dot_nt(a, b):
    return lax.dot_general(a, b, (((1,), (1,)), ((), ())), preferred_element_type=F32)


def column(row):
    return jnp.broadcast_to(row, (128, 128)).T


def lanes(x, idx):
    return jnp.take_along_axis(x, idx, axis=1, mode="promise_in_bounds")


def onehot(rows, code):
    ids = iota((rows, 128), 0).astype(F32).astype(BF)
    return jnp.where(ids == jnp.broadcast_to(code, (rows, 128)).astype(BF), jnp.ones((), BF), jnp.zeros((), BF)).astype(F8)


def codes(src_ref, vec_ref, len_ref, hi0, hi1, lo):
    parts = []
    for b in range(4):
        rows = pl.ds(128 * b, 128)
        used = iota((128, 64), 1) < column(len_ref[pl.ds(b, 1), :].astype(F32))[:, :64].astype(I32)
        src = src_ref[rows, :]
        high = jnp.where(used, vec_ref[rows, :] + 16 * (src >> 8), -1).astype(F32)
        parts.append((high, (src & 255).astype(F32)))
    for b in range(2):
        rows = pl.ds(128 * b, 128)
        high = jnp.concatenate([parts[b][0], parts[b + 2][0]], 1)
        first = iota((128, 128), 1) < 64
        hi0[rows, :] = jnp.where(first, high, -1.0)
        hi1[rows, :] = jnp.where(first, -1.0, high)
        lo[rows, :] = jnp.concatenate([parts[b][1], parts[b + 2][1]], 1)


def count_pair(p, hi0, hi1, lo, S):
    a = jnp.concatenate([onehot(160, hi0[pl.ds(p, 1), :]), onehot(160, hi1[pl.ds(p, 1), :])], 0)
    s = dot_nt(a, onehot(256, lo[pl.ds(p, 1), :])).astype(BF)
    for t in range(10):
        S[t, p] = s[16 * t : 16 * t + 16]
        S[t, p + 256] = s[160 + 16 * t : 176 + 16 * t]


def near_prepare(E, near_ref, XT, Y, tgt, src):
    for f in range(4):
        for h in range(2):
            XT[f, h] = E[f, pl.ds(128 * h, 128), :].T
        own = E[f, pl.ds(8, 128), :].T if f < 3 else None
        lane = iota((32, 128), 1)
        for b in range(5):
            y = None
            for q in range(4):
                g = lanes(XT[f, b // 4, pl.ds(32 * q, 32), :], 32 * (b % 4) + (lane >> 2))
                y = g if q == 0 else jnp.where((lane & 3) == q, g, y)
            Y[f, b] = y
        if f < 3:
            for b in range(4):
                y = None
                for q in range(4):
                    g = lanes(own[32 * q : 32 * q + 32], 32 * b + (lane >> 2))
                    y = g if q == 0 else jnp.where((lane & 3) == q, g, y)
                tgt[b, f] = y
    for b in range(4):
        listed = near_ref[pl.ds(128 * b, 128), :].astype(F32)
        listed = jnp.concatenate([listed, jnp.zeros((128, 120), F32)], 1).T
        for n in range(8):
            idx = jnp.broadcast_to(listed[n : n + 1].astype(I32) - 128 * b, (32, 128))
            inside, wrapped = idx < 128, idx & 127
            for f in range(4):
                g = jnp.where(inside, lanes(Y[f, b], wrapped), lanes(Y[f, b + 1], wrapped))
                for s in range(4):
                    src[b, 4 * n + s, f] = g[8 * s : 8 * s + 8]


def near_unit(b, jj, J, tgt, src, N):
    ts = [
        [jnp.broadcast_to(tgt[b, f, pl.ds(jj * J + j, 1), :], (8, 128)) for f in range(3)] for j in range(J)
    ]
    acc = [jnp.zeros((8, 128), F32) for _ in range(J)]
    for m in range(32):
        x, y, z, q = (src[b, m, f] for f in range(4))
        for j in range(J):
            dx, dy, dz = x - ts[j][0], y - ts[j][1], z - ts[j][2]
            acc[j] = acc[j] + q * lax.rsqrt(dx * dx + dy * dy + (dz * dz + SOFT))
    for j in range(J):
        N[b, pl.ds(jj * J + j, 1), :] = jnp.sum(acc[j], 0, keepdims=True)


def near_rows(N):
    lane = iota((32, 128), 1)
    parts = []
    for q in range(4):
        z = None
        for b in range(4):
            g = lanes(N[b], 4 * (lane & 31) + q)
            z = g if b == 0 else jnp.where((lane >> 5) == b, g, z)
        parts.append(z)
    return jnp.concatenate(parts, 0).T


def group(i, n, table, S, G, Gb):
    rows = 16 * n
    lhs = jnp.concatenate([S[t, pl.ds(i * n, n)].reshape(rows, 256) for t in range(10)], 1)
    g = dot(lhs, table[...])
    G[0] = g[:, :128]
    G[1] = g[:, 128:]
    for v in range(16):
        Gb[v, pl.ds(i * n, n), :] = jnp.concatenate(
            [G[0, pl.ds(v, n, stride=16), :], G[1, pl.ds(v, n, stride=16), :]], 1
        ).astype(BF)


def coarse_rows(parent_ref, octant_ref, coarse, Gb):
    for b in range(4):
        parent = column(parent_ref[pl.ds(b, 1), :].astype(F32))
        octant = column(octant_ref[pl.ds(b, 1), :].astype(F32))
        lane = iota((128, 128), 1).astype(F32)
        pick = jnp.concatenate([(parent == lane).astype(F32), (parent == lane + 128.0).astype(F32)], 1).astype(BF)
        rows = dot(pick, coarse[...])
        octant = jnp.concatenate([octant, octant], 1)
        for o in range(8):
            Gb[16 + o, pl.ds(128 * b, 128), :] = jnp.where(octant == float(o), rows, 0.0).astype(BF)


def far_rows(i, S, rounded, F):
    pieces = []
    for c in range(16):
        pieces += [S[0, i * 16 + c], S[1, i * 16 + c]]
    r = dot_nt(rounded[pl.ds(pl.multiple_of(16 * i, 16), 16), :], jnp.concatenate(pieces, 0))
    r = jnp.where(iota((16, 512), 0) == (iota((16, 512), 1) >> 5), r, 0.0)
    r = jnp.sum(r, 0, keepdims=True)
    for h in range(4):
        F[pl.ds(4 * i + h, 1), :] = r[:, 128 * h : 128 * h + 128]


NBLK = 64


def kernel(
    table_ref, coarse_ref, src_ref, vec_ref, len_ref, parent_ref, octant_ref, near_ref, ext_ref, m2l_hbm, l2l_hbm, basis_hbm,
    leaf_ref, pot_ref,
    S, G, Gb, ops, rounded, hi0, hi1, lo, XT, Y, tgt, src, N, F, sem_ops, sem_basis,
):
    ops_in = [
        pltpu.make_async_copy(m2l_hbm, ops.at[pl.ds(0, 16)], sem_ops.at[0]),
        pltpu.make_async_copy(l2l_hbm, ops.at[pl.ds(16, 8)], sem_ops.at[1]),
    ]
    for c in ops_in:
        c.start()
    codes(src_ref, vec_ref, len_ref, hi0, hi1, lo)
    lax.fori_loop(0, 256, lambda p, _: count_pair(p, hi0, hi1, lo, S), None, unroll=32)
    near_prepare(ext_ref, near_ref, XT, Y, tgt, src)
    for b in range(4):
        lax.fori_loop(0, 8, lambda jj, _: near_unit(b, jj, 4, tgt, src, N), None)
    coarse_rows(parent_ref, octant_ref, coarse_ref, Gb)

    def basis_copy(i, h):
        cells = pl.ds(i * NBLK, NBLK)
        return pltpu.make_async_copy(basis_hbm.at[cells, h], S.at[h, cells], sem_basis.at[i, h])

    def block(i, _):
        group(i, NBLK, table_ref, S, G, Gb)
        basis_copy(i, 0).start()
        basis_copy(i, 1).start()

    lax.fori_loop(0, 512 // NBLK, block, None)
    for c in ops_in:
        c.wait()
    for h in range(2):
        rows = pl.ds(256 * h, 256)
        leaf = dot(
            jnp.concatenate([Gb[v, rows, :] for v in range(24)], 1), ops[...].reshape(24 * 256, 256)
        )
        leaf_ref[rows, :] = leaf
        rounded[rows, :] = leaf.astype(BF)
    for i in range(512 // NBLK):
        basis_copy(i, 0).wait()
        basis_copy(i, 1).wait()
    lax.fori_loop(0, 32, lambda i, _: far_rows(i, S, rounded, F), None, unroll=4)
    pot_ref[...] = F[...] + near_rows(N)


def call(table, coarse, src, vec, length, parent, octant, near, ext, m2l, l2l, basis):
    vmem = pl.BlockSpec(memory_space=pltpu.VMEM)
    hbm = pl.BlockSpec(memory_space=pl.ANY)
    return pl.pallas_call(
        kernel,
        out_shape=(jax.ShapeDtypeStruct((512, 256), F32), jax.ShapeDtypeStruct((128, 128), F32)),
        in_specs=[vmem] * 9 + [hbm] * 3,
        out_specs=(vmem, vmem),
        scratch_shapes=[
            pltpu.VMEM((10, 512, 16, 256), BF),
            pltpu.VMEM((2, 16 * NBLK, 128), F32),
            pltpu.VMEM((24, 512, 256), BF),
            pltpu.VMEM((24, 256, 256), BF),
            pltpu.VMEM((512, 256), BF),
            pltpu.VMEM((256, 128), F32),
            pltpu.VMEM((256, 128), F32),
            pltpu.VMEM((256, 128), F32),
            pltpu.VMEM((4, 2, 128, 128), F32),
            pltpu.VMEM((4, 5, 32, 128), F32),
            pltpu.VMEM((4, 3, 32, 128), F32),
            pltpu.VMEM((4, 32, 4, 8, 128), F32),
            pltpu.VMEM((4, 32, 128), F32),
            pltpu.VMEM((128, 128), F32),
            pltpu.SemaphoreType.DMA((2,)),
            pltpu.SemaphoreType.DMA((512 // NBLK, 2)),
        ],
        compiler_params=pltpu.CompilerParams(vmem_limit_bytes=63 << 20),
    )(table, coarse, src, vec, length, parent, octant, near, ext, m2l, l2l, basis.reshape(512, 2, 16, 256))


def shifted_2(shard, axis, by):
    peers = lax.axis_size(axis)
    pairs = [(i, i + by) for i in range(peers) if 0 <= i + by < peers]
    return lax.ppermute(shard, axis, pairs)


def shards(multipole, coarse_local, send_rows, list_src, list_vec, list_len, parent_of, octant, m2l_ops, l2l_ops, near_list, positions, charges, basis):
    ids = send_rows.reshape(-1)
    pick = (ids[:, None] == jnp.arange(512, dtype=I32)[None, :]).astype(BF)
    outgoing = dot(pick, multipole).astype(BF).reshape(128, 16, 256)
    incoming = lax.all_to_all(outgoing, ("gx", "gy"), split_axis=0, concat_axis=0, tiled=True)
    table = jnp.concatenate([multipole, incoming.reshape(-1, 256)], axis=0)
    whole = lax.all_gather(coarse_local, "gx", axis=0, tiled=True)
    data = jnp.concatenate([positions, charges[None, :]], axis=0).reshape(4, 128, 128)
    lower = shifted_2(data[:, 120:], ("gx", "gy"), 1)
    upper = shifted_2(data[:, :8], ("gx", "gy"), -1)
    ext = jnp.concatenate([lower, data, upper, jnp.zeros((4, 112, 128), F32)], axis=1)
    leaf, pot = call(
        table, whole, list_src, list_vec, list_len.reshape(4, 128), parent_of.reshape(4, 128), octant.reshape(4, 128),
        near_list, ext, m2l_ops, l2l_ops, basis,
    )
    return leaf, pot.reshape(-1)


def solution(mesh):
    both = ("gx", "gy")
    placed = (
        P(both, None), P("gx", None), P(both, None, None), P(both, None), P(both, None), P(both), P(both), P(both),
        P(), P(), P(both, None), P(None, both), P(both), P(both, None),
    )
    return jax.shard_map(shards, mesh=mesh, in_specs=placed, out_specs=(P(both, None), P(both)), check_vma=False)
```

time: 299 us -> 83.2 us (0.28)
  local copies, waits for them, and re-layouts: 204 us -> 3.52 us
  Pallas kernels: 0 us -> 37.9 us
  other arithmetic: 27.3 us -> 2.07 us
  matrix products: 25.1 us -> 2.87 us
  blocking collectives: 21.3 us -> 14.6 us
  starting transfers between devices: 17.8 us -> 21.1 us
    gather x14 -> x0, local copies, waits for them, and re-layouts: 169 us -> none  [the longest x4 132 us: translate(): rows = table[src]]
    pallas_call x0 -> x1, Pallas kernels: none -> 37.9 us  [call(): pl.pallas_call(kernel, out_shape=(jax.ShapeDtypeStruct((512, 256), F32),...]
    dot_general x10 -> x1, matrix products: 25.1 us -> 2.87 us  [dot(): return jnp.dot(a, b, preferred_element_type=F32)]
    reduce_sum x4 -> x0, other arithmetic: 14.1 us -> none  [near_sum(): return jnp.sum(tiles[3][:, None, :] * lax.rsqrt(total + softening), axis=2)]
    dynamic_slice x8 -> x0, local copies, waits for them, and re-layouts: 7.56 us -> none  [the longest x4 3.8 us: shards(): lax.map(near_block, (near_list.reshape(near_blocks, near_block_size, -1),...]
    select_n x10 -> x0, other arithmetic: 6.82 us -> none  [the longest x4 3.42 us: translate(): rows = table[src]]
    all_gather x1, blocking collectives: 21.3 us -> 14.6 us  [shards(): whole = lax.all_gather(coarse_local, 'gx', axis=0, tiled=True)]
    all_to_all x1, starting transfers between devices: 6.38 us -> 11.5 us  [shards(): lax.all_to_all(outgoing, ('gx', 'gy'), split_axis=0, concat_axis=0, tiled...]
  transfers between devices with their start and end apart: 3 -> 3, of which waited for: 0 -> 0; matrix products, arithmetic and copies ran while one was open for 28% -> 4% of each run, Pallas kernels for 0% -> 0%
where the time goes in v1:
time: 83.2 us; the launch traced here: 82.9 us
  Pallas kernels  37.9 us (46%)
  starting transfers between devices  21.1 us (25%)
  blocking collectives  14.6 us (18%)
  local copies, waits for them, and re-layouts  3.52 us (4%)
  matrix products  2.87 us (3%)
  other arithmetic  2.07 us (2%)
    pallas_call x1, Pallas kernels, call(): pl.pallas_call(kernel, out_shape=(jax.ShapeDtypeStruct((512, 256), F32),...  37.9 us
    all_gather x1, blocking collectives, shards(): whole = lax.all_gather(coarse_local, 'gx', axis=0, tiled=True)  14.6 us
    all_to_all x1, starting transfers between devices, shards(): lax.all_to_all(outgoing, ('gx', 'gy'), split_axis=0, concat_axis=0, tiled...  11.5 us
    ppermute x2, starting transfers between devices, shifted_2(): return lax.ppermute(shard, axis, pairs)  9.64 us
    unnamed x19, local copies, waits for them, and re-layouts  3.36 us
    dot_general x1, matrix products, dot(): return jnp.dot(a, b, preferred_element_type=F32)  2.87 us
  transfers between devices with their start and end apart: 3, of which 0 were waited for; matrix products, arithmetic and copies ran while one was open for 4% of the time, Pallas kernels for 0%

profile of v1, /device:TPU:1, one launch (start us, length us, event | category | flops | bytes accessed | tf_op | source)
XLA Modules:
  0.0 82.9 jit_solution(12850618090893569054)
XLA Ops:
  0.6 0.8 copy.19
  1.4 0.1 eq.15
  1.5 0.0 copy-start.1
  1.5 0.0 copy-start.2
  1.5 2.9 %fusion.1 = bf16[2048,256]{1,0:T(8,128)(2,1)} fusion(bf16[512,256]{1,0:T(8,128)(2,1)} %param.14, s32[2048]{0:T(1024)S(1)} %eq.15), kind=kOutput, calls=%fused_computation.2 | convolution fusion | flops 538443776 | bytes 1318912 | tf_op jit(solution)/shard_map/dot_general | solution.py:22
  4.4 0.0 copy-start.5
  4.4 0.0 copy-start.3
  4.4 0.0 copy-start.4
  4.4 0.0 copy-start.6
  4.4 0.0 copy-start
  4.4 11.5 %all-to-all-start = ((bf16[128,16,256]{2,1,0:T(8,128)(2,1)}), bf16[128,16,256]{2,1,0:T(8,128)(2,1)S(1)}, u32[]{:S(2)}, u32[]{:S(2)}) async-start(bf16[128,16,256]{2,1,0:T(8,128)(2,1)} %bitcast), calls=%async_computation | async-start | bytes 2097152 | tf_op jit(solution)/shard_map/all_to_all | solution.py:246
  15.9 0.0 copy-done.1
  16.0 0.0 copy-done.2
  16.0 3.3 %collective-permute-start = (f32[4,8,128]{2,1,0:T(8,128)S(1)}, f32[4,8,128]{2,1,0:T(8,128)S(1)}, u32[]{:S(2)}, u32[]{:S(2)}) collective-permute-start(f32[4,8,128]{2,1,0:T(8,128)S(1)} %get-tuple-element.6), channel_id=1, source_target_pairs={{0,1},{1,2},{2,3},{3,4},{4,5},{5,6},{6,7},{7,8},{8,9},{9,10},{10,1... | collective-permute-start | bytes 49160 | tf_op jit(solution)/shard_map/ppermute | solution.py:239
  19.3 6.3 %collective-permute-start.1 = (f32[4,8,128]{2,1,0:T(8,128)S(1)}, f32[4,8,128]{2,1,0:T(8,128)S(1)}, u32[]{:S(2)}, u32[]{:S(2)}) collective-permute-start(f32[4,8,128]{2,1,0:T(8,128)S(1)} %get-tuple-element.7), channel_id=1, source_target_pairs={{1,0},{2,1},{3,2},{4,3},{5,4},{6,5},{7,6},{8,7},{9,8},{10,9},{11,1... | collective-permute-start | bytes 49160 | tf_op jit(solution)/shard_map/ppermute | solution.py:239
  25.6 0.0 copy-done.5
  25.7 14.6 %all_gather.3.coarse_ref = bf16[256,256]{1,0:T(8,128)(2,1)} all-gather(bf16[32,256]{1,0:T(8,128)(2,1)S(1)} %copy-done.5), channel_id=1, replica_groups=mesh['gx'=8,'gy'=16] {'gx'}, dimensions={0}, use_global_device_ids=true | all-gather | bytes 147456 | tf_op jit(solution)/shard_map/all_gather | solution.py:248
  40.3 0.0 copy-done.3
  40.3 0.9 %copy.20.src_ref = s32[512,64]{1,0:T(8,128)} copy(s32[512,64]{0,1:T(8,128)S(1)} %copy-done.3) | data formatting | bytes 262144 | tf_op args[3]
  41.2 0.0 copy-done.4
  41.2 0.8 copy.21.vec_ref
  42.0 0.0 copy-done.6
  42.0 0.8 %copy.22.near_ref = s32[512,8]{1,0:T(8,128)} copy(s32[512,8]{0,1:T(8,128)S(1)} %copy-done.6) | data formatting | bytes 32768 | tf_op args[10]
  42.8 0.1 pad.4.clone
  42.9 0.0 collective-permute-done
  42.9 0.0 collective-permute-done.1
  42.9 0.9 %maximum_maximum_fusion.ext_ref = f32[4,256,128]{2,1,0:T(8,128)} fusion(f32[4,8,128]{2,1,0:T(8,128)S(1)} %collective-permute-done.1, f32[1,128,128]{2,1,0:T(8,128)S(1)} %bitcast.19, f32[3,128,128]{2,1,0:T(8,128)S(1)} %bitcast.16, f32[4,8,128]{2,1,0:T(8,128)S(1)} %collective-permute-done, f32[256]{0:T(256)S(1)} %pad.4.clone), kind=kLoop, calls=%fused_computation.5 | loop fusion | flops 524288 | bytes 820224 | tf_op jit(solution)/shard_map/concatenate | solution.py:252
  43.8 0.0 all-to-all-done
  43.8 0.0 copy-done
  43.8 1.2 %pad_maximum_fusion.table_ref = bf16[2560,256]{1,0:T(8,128)(2,1)} fusion(bf16[2048,256]{1,0:T(8,128)(2,1)S(1)} %bitcast.14, bf16[512,256]{1,0:T(8,128)(2,1)S(1)} %copy-done), kind=kLoop, calls=%fused_computation.4 | loop fusion | flops 2621440 | bytes 2621440 | tf_op jit(solution)/shard_map/concatenate | solution.py:247
  45.0 37.9 %shard_map.149 = (f32[512,256]{1,0:T(8,128)}, f32[128,128]{1,0:T(8,128)}) custom-call(bf16[2560,256]{1,0:T(8,128)(2,1)} %pad_maximum_fusion.table_ref, bf16[256,256]{1,0:T(8,128)(2,1)} %all_gather.3.coarse_ref, s32[512,64]{1,0:T(8,128)} %copy.20.src_ref, s32[512,64]{1,0:T(8,128)} %copy.21.vec_ref, s32[4,128]{1,0:T(4,128)} %bitcast.20, s32[4,128]{1,0:T(4,128)} %bitcast.21, ...), custom_call_target="tpu_custom_call" | custom-call | tf_op jit(solution)/shard_map/pallas_call | solution.py:209
  (3 shorter events, 0.0 us)
Async XLA Ops:
  1.5 14.4 %copy-start.1 = (f32[3,16384]{1,0:T(4,128)S(1)}, f32[3,16384]{1,0:T(4,128)}, u32[]{:S(2)}) copy-start(f32[3,16384]{1,0:T(4,128)} %param.25) | copy-start | bytes 589828
  1.5 14.4 %copy-start.2 = (f32[16384]{0:T(1024)S(1)}, f32[16384]{0:T(1024)}, u32[]{:S(2)}) copy-start(f32[16384]{0:T(1024)} %param.26) | copy-start | bytes 196612
  4.4 21.3 %copy-start.5 = (bf16[32,256]{1,0:T(8,128)(2,1)S(1)}, bf16[32,256]{1,0:T(8,128)(2,1)}, u32[]{:S(2)}) copy-start(bf16[32,256]{1,0:T(8,128)(2,1)} %param.15) | copy-start | bytes 49156
  4.4 35.9 %copy-start.3 = (s32[512,64]{0,1:T(8,128)S(1)}, s32[512,64]{0,1:T(8,128)}, u32[]{:S(2)}) copy-start(s32[512,64]{0,1:T(8,128)} %param.17) | copy-start | bytes 393220
  4.4 36.8 %copy-start.4 = (s32[512,64]{0,1:T(8,128)S(1)}, s32[512,64]{0,1:T(8,128)}, u32[]{:S(2)}) copy-start(s32[512,64]{0,1:T(8,128)} %param.18) | copy-start | bytes 393220
  4.4 37.6 %copy-start.6 = (s32[512,8]{0,1:T(8,128)S(1)}, s32[512,8]{0,1:T(8,128)}, u32[]{:S(2)}) copy-start(s32[512,8]{0,1:T(8,128)} %param.24) | copy-start | bytes 49156
  4.4 39.4 %copy-start = (bf16[512,256]{1,0:T(8,128)(2,1)S(1)}, bf16[512,256]{1,0:T(8,128)(2,1)}, u32[]{:S(2)}) copy-start(bf16[512,256]{1,0:T(8,128)(2,1)} %param.14) | copy-start | bytes 786436
  4.4 39.4 %all-to-all-start = ((bf16[128,16,256]{2,1,0:T(8,128)(2,1)}), bf16[128,16,256]{2,1,0:T(8,128)(2,1)S(1)}, u32[]{:S(2)}, u32[]{:S(2)}) async-start(bf16[128,16,256]{2,1,0:T(8,128)(2,1)} %bitcast), calls=%async_computation | async-start | bytes 2097152 | tf_op jit(solution)/shard_map/all_to_all | solution.py:246
  16.0 26.9 %collective-permute-start = (f32[4,8,128]{2,1,0:T(8,128)S(1)}, f32[4,8,128]{2,1,0:T(8,128)S(1)}, u32[]{:S(2)}, u32[]{:S(2)}) collective-permute-start(f32[4,8,128]{2,1,0:T(8,128)S(1)} %get-tuple-element.6), channel_id=1, source_target_pairs={{0,1},{1,2},{2,3},{3,4},{4,5},{5,6},{6,7},{7,8},{8,9},{9,10},{10,1... | collective-permute-start | bytes 49160 | tf_op jit(solution)/shard_map/ppermute | solution.py:239
  19.3 23.6 %collective-permute-start.1 = (f32[4,8,128]{2,1,0:T(8,128)S(1)}, f32[4,8,128]{2,1,0:T(8,128)S(1)}, u32[]{:S(2)}, u32[]{:S(2)}) collective-permute-start(f32[4,8,128]{2,1,0:T(8,128)S(1)} %get-tuple-element.7), channel_id=1, source_target_pairs={{1,0},{2,1},{3,2},{4,3},{5,4},{6,5},{7,6},{8,7},{9,8},{10,9},{11,1... | collective-permute-start | bytes 49160 | tf_op jit(solution)/shard_map/ppermute | solution.py:239

commit v2 on v1

--- a/solution.py
+++ b/solution.py
@@ -42,18 +42,18 @@
 def codes(src_ref, vec_ref, len_ref, hi0, hi1, lo):
     parts = []
     for b in range(4):
-        rows = pl.ds(128 * b, 128)
-        used = iota((128, 64), 1) < column(len_ref[pl.ds(b, 1), :].astype(F32))[:, :64].astype(I32)
-        src = src_ref[rows, :]
-        high = jnp.where(used, vec_ref[rows, :] + 16 * (src >> 8), -1).astype(F32)
+        cells = pl.ds(128 * b, 128)
+        used = iota((64, 128), 0) < len_ref[pl.ds(b, 1), :]
+        src = src_ref[:, cells]
+        high = jnp.where(used, vec_ref[:, cells] + 16 * (src >> 8), -1).astype(F32)
         parts.append((high, (src & 255).astype(F32)))
+    first = iota((128, 128), 1) < 64
     for b in range(2):
         rows = pl.ds(128 * b, 128)
-        high = jnp.concatenate([parts[b][0], parts[b + 2][0]], 1)
-        first = iota((128, 128), 1) < 64
+        high = jnp.concatenate([parts[b][0], parts[b + 2][0]], 0).T
         hi0[rows, :] = jnp.where(first, high, -1.0)
         hi1[rows, :] = jnp.where(first, -1.0, high)
-        lo[rows, :] = jnp.concatenate([parts[b][1], parts[b + 2][1]], 1)
+        lo[rows, :] = jnp.concatenate([parts[b][1], parts[b + 2][1]], 0).T
 
 
 def count_pair(p, hi0, hi1, lo, S):
@@ -84,10 +84,9 @@
                     y = g if q == 0 else jnp.where((lane & 3) == q, g, y)
                 tgt[b, f] = y
     for b in range(4):
-        listed = near_ref[pl.ds(128 * b, 128), :].astype(F32)
-        listed = jnp.concatenate([listed, jnp.zeros((128, 120), F32)], 1).T
+        listed = near_ref[:, pl.ds(128 * b, 128)]
         for n in range(8):
-            idx = jnp.broadcast_to(listed[n : n + 1].astype(I32) - 128 * b, (32, 128))
+            idx = jnp.broadcast_to(listed[n : n + 1] - 128 * b, (32, 128))
             inside, wrapped = idx < 128, idx & 127
             for f in range(4):
                 g = jnp.where(inside, lanes(Y[f, b], wrapped), lanes(Y[f, b + 1], wrapped))
@@ -121,10 +120,10 @@
     return jnp.concatenate(parts, 0).T
 
 
-def group(i, n, table, S, G, Gb):
+def group(i, n, own, incoming, S, G, Gb):
     rows = 16 * n
-    lhs = jnp.concatenate([S[t, pl.ds(i * n, n)].reshape(rows, 256) for t in range(10)], 1)
-    g = dot(lhs, table[...])
+    lhs = [S[t, pl.ds(i * n, n)].reshape(rows, 256) for t in range(10)]
+    g = dot(jnp.concatenate(lhs[:2], 1), own[...]) + dot(jnp.concatenate(lhs[2:], 1), incoming[...].reshape(2048, 256))
     G[0] = g[:, :128]
     G[1] = g[:, 128:]
     for v in range(16):
@@ -139,7 +138,7 @@
         octant = column(octant_ref[pl.ds(b, 1), :].astype(F32))
         lane = iota((128, 128), 1).astype(F32)
         pick = jnp.concatenate([(parent == lane).astype(F32), (parent == lane + 128.0).astype(F32)], 1).astype(BF)
-        rows = dot(pick, coarse[...])
+        rows = dot(pick, coarse[...].reshape(256, 256))
         octant = jnp.concatenate([octant, octant], 1)
         for o in range(8):
             Gb[16 + o, pl.ds(128 * b, 128), :] = jnp.where(octant == float(o), rows, 0.0).astype(BF)
@@ -156,33 +155,132 @@
         F[pl.ds(4 * i + h, 1), :] = r[:, 128 * h : 128 * h + 128]
 
 
+def fill_data(pos_ref, charge_ref, E):
+    for r in range(128):
+        for f in range(3):
+            E[f, pl.ds(8 + r, 1), :] = pos_ref[pl.ds(f, 1), pl.ds(128 * r, 128)]
+    E[3, pl.ds(8, 128), :] = charge_ref[...]
+
+
+def pick_rows(send_ref, multipole, SG, outgoing):
+    lane = iota((128, 128), 1).astype(F32)
+    for jj in range(4):
+        picks = []
+        for j in range(4):
+            ids = column(send_ref[pl.ds(4 * jj + j, 1), :].astype(F32))
+            picks.append(jnp.concatenate([(ids == lane + 128.0 * h).astype(F32).astype(BF) for h in range(4)], 1))
+        rows = dot(jnp.concatenate(picks, 0), multipole[...])
+        SG[0, pl.ds(512 * jj, 512), :] = rows[:, :128]
+        SG[1, pl.ds(512 * jj, 512), :] = rows[:, 128:]
+    for d in range(128):
+        rows = pl.ds(d, 16, stride=128)
+        outgoing[d] = jnp.concatenate([SG[0, rows, :], SG[1, rows, :]], 1).astype(BF)
+
+
 NBLK = 64
+MESH = pl.DeviceIdType.MESH
 
 
 def kernel(
-    table_ref, coarse_ref, src_ref, vec_ref, len_ref, parent_ref, octant_ref, near_ref, ext_ref, m2l_hbm, l2l_hbm, basis_hbm,
+    multipole_ref, coarse_ref, send_ref, src_ref, vec_ref, len_ref, parent_ref, octant_ref, near_ref, pos_ref, charge_ref,
+    m2l_hbm, l2l_hbm, basis_hbm,
     leaf_ref, pot_ref,
-    S, G, Gb, ops, rounded, hi0, hi1, lo, XT, Y, tgt, src, N, F, sem_ops, sem_basis,
+    S, G, Gb, ops, rounded, hi0, hi1, lo, XT, Y, tgt, src, N, F, E, SG, outgoing, incoming, coarse,
+    sem_ops, sem_basis, send_sem, recv_sem, coarse_send, coarse_recv, rim_send, rim_recv,
 ):
+    gx, gy = lax.axis_index("gx"), lax.axis_index("gy")
+    me = gx * 16 + gy
+    E[:, pl.ds(0, 8), :] = jnp.zeros((4, 8, 128), F32)
+    E[:, pl.ds(136, 120), :] = jnp.zeros((4, 120, 128), F32)
+
+    barrier = pltpu.get_barrier_semaphore()
+
+    def greet(o, _):
+        d = lax.rem(me + o, 128)
+        pl.semaphore_signal(barrier, inc=1, device_id=(d // 16, lax.rem(d, 16)), device_id_type=MESH)
+
+    lax.fori_loop(1, 128, greet, None)
     ops_in = [
         pltpu.make_async_copy(m2l_hbm, ops.at[pl.ds(0, 16)], sem_ops.at[0]),
         pltpu.make_async_copy(l2l_hbm, ops.at[pl.ds(16, 8)], sem_ops.at[1]),
     ]
     for c in ops_in:
         c.start()
+    fill_data(pos_ref, charge_ref, E)
+    pick_rows(send_ref, multipole_ref, SG, outgoing)
+    pl.semaphore_wait(barrier, 127)
+
+    def send(o):
+        d = lax.rem(me + o, 128)
+        return pltpu.make_async_remote_copy(
+            src_ref=outgoing.at[d], dst_ref=incoming.at[me], send_sem=send_sem, recv_sem=recv_sem,
+            device_id=(d // 16, lax.rem(d, 16)), device_id_type=MESH,
+        )
+
+    def send_coarse(r):
+        return pltpu.make_async_remote_copy(
+            src_ref=coarse_ref, dst_ref=coarse.at[gx], send_sem=coarse_send, recv_sem=coarse_recv,
+            device_id=(lax.rem(gx + r, 8), gy), device_id_type=MESH,
+        )
+
+    def send_rim(up):
+        d = me + 1 if up else me - 1
+        return pltpu.make_async_remote_copy(
+            src_ref=E.at[:, pl.ds(128 if up else 8, 8)], dst_ref=E.at[:, pl.ds(0 if up else 136, 8)],
+            send_sem=rim_send.at[int(up)], recv_sem=rim_recv.at[int(up)],
+            device_id=(d // 16, lax.rem(d, 16)), device_id_type=MESH,
+        )
+
+    @pl.when(me < 127)
+    def _():
+        send_rim(True).start()
+
+    @pl.when(me > 0)
+    def _():
+        send_rim(False).start()
+
+    lax.fori_loop(1, 128, lambda o, _: send(o).start(), None)
+    lax.fori_loop(1, 8, lambda r, _: send_coarse(r).start(), None)
+    incoming[me] = outgoing[me]
+    coarse[gx] = coarse_ref[...]
+
     codes(src_ref, vec_ref, len_ref, hi0, hi1, lo)
     lax.fori_loop(0, 256, lambda p, _: count_pair(p, hi0, hi1, lo, S), None, unroll=32)
-    near_prepare(ext_ref, near_ref, XT, Y, tgt, src)
+
+    @pl.when(me > 0)
+    def _():
+        send_rim(True).wait_recv()
+        send_rim(False).wait_send()
+
+    @pl.when(me < 127)
+    def _():
+        send_rim(False).wait_recv()
+        send_rim(True).wait_send()
+
+    near_prepare(E, near_ref, XT, Y, tgt, src)
     for b in range(4):
         lax.fori_loop(0, 8, lambda jj, _: near_unit(b, jj, 4, tgt, src, N), None)
-    coarse_rows(parent_ref, octant_ref, coarse_ref, Gb)
+
+    def all_of(ref, n, send_sem, recv_sem):
+        part = ref.at[pl.ds(0, n)]
+        return pltpu.make_async_remote_copy(
+            src_ref=part, dst_ref=part, send_sem=send_sem, recv_sem=recv_sem, device_id=(gx, gy), device_id_type=MESH
+        )
+
+    coarse_in = all_of(coarse, 7, coarse_send, coarse_recv)
+    coarse_in.wait_send()
+    coarse_in.wait_recv()
+    coarse_rows(parent_ref, octant_ref, coarse, Gb)
+    rows_in = all_of(incoming, 127, send_sem, recv_sem)
+    rows_in.wait_send()
+    rows_in.wait_recv()
 
     def basis_copy(i, h):
         cells = pl.ds(i * NBLK, NBLK)
         return pltpu.make_async_copy(basis_hbm.at[cells, h], S.at[h, cells], sem_basis.at[i, h])
 
     def block(i, _):
-        group(i, NBLK, table_ref, S, G, Gb)
+        group(i, NBLK, multipole_ref, incoming, S, G, Gb)
         basis_copy(i, 0).start()
         basis_copy(i, 1).start()
 
@@ -191,9 +289,7 @@
         c.wait()
     for h in range(2):
         rows = pl.ds(256 * h, 256)
-        leaf = dot(
-            jnp.concatenate([Gb[v, rows, :] for v in range(24)], 1), ops[...].reshape(24 * 256, 256)
-        )
+        leaf = dot(jnp.concatenate([Gb[v, rows, :] for v in range(24)], 1), ops[...].reshape(24 * 256, 256))
         leaf_ref[rows, :] = leaf
         rounded[rows, :] = leaf.astype(BF)
     for i in range(512 // NBLK):
@@ -203,13 +299,17 @@
     pot_ref[...] = F[...] + near_rows(N)
 
 
-def call(table, coarse, src, vec, length, parent, octant, near, ext, m2l, l2l, basis):
+def shards(
+    multipole, coarse_local, send_rows, list_src, list_vec, list_len, parent_of, octant, m2l_ops, l2l_ops, near_list,
+    positions, charges, basis,
+):
     vmem = pl.BlockSpec(memory_space=pltpu.VMEM)
     hbm = pl.BlockSpec(memory_space=pl.ANY)
-    return pl.pallas_call(
+    dma = pltpu.SemaphoreType.DMA
+    leaf, pot = pl.pallas_call(
         kernel,
         out_shape=(jax.ShapeDtypeStruct((512, 256), F32), jax.ShapeDtypeStruct((128, 128), F32)),
-        in_specs=[vmem] * 9 + [hbm] * 3,
+        in_specs=[vmem] * 11 + [hbm] * 3,
         out_specs=(vmem, vmem),
         scratch_shapes=[
             pltpu.VMEM((10, 512, 16, 256), BF),
@@ -226,33 +326,18 @@
             pltpu.VMEM((4, 32, 4, 8, 128), F32),
             pltpu.VMEM((4, 32, 128), F32),
             pltpu.VMEM((128, 128), F32),
-            pltpu.SemaphoreType.DMA((2,)),
-            pltpu.SemaphoreType.DMA((512 // NBLK, 2)),
+            pltpu.VMEM((4, 256, 128), F32),
+            pltpu.VMEM((2, 2048, 128), F32),
+            pltpu.VMEM((128, 16, 256), BF),
+            pltpu.VMEM((128, 16, 256), BF),
+            pltpu.VMEM((8, 32, 256), BF),
+            dma((2,)), dma((512 // NBLK, 2)), dma, dma, dma, dma, dma((2,)), dma((2,)),
         ],
-        compiler_params=pltpu.CompilerParams(vmem_limit_bytes=63 << 20),
-    )(table, coarse, src, vec, length, parent, octant, near, ext, m2l, l2l, basis.reshape(512, 2, 16, 256))
-
-
-def shifted_2(shard, axis, by):
-    peers = lax.axis_size(axis)
-    pairs = [(i, i + by) for i in range(peers) if 0 <= i + by < peers]
-    return lax.ppermute(shard, axis, pairs)
-
-
-def shards(multipole, coarse_local, send_rows, list_src, list_vec, list_len, parent_of, octant, m2l_ops, l2l_ops, near_list, positions, charges, basis):
-    ids = send_rows.reshape(-1)
-    pick = (ids[:, None] == jnp.arange(512, dtype=I32)[None, :]).astype(BF)
-    outgoing = dot(pick, multipole).astype(BF).reshape(128, 16, 256)
-    incoming = lax.all_to_all(outgoing, ("gx", "gy"), split_axis=0, concat_axis=0, tiled=True)
-    table = jnp.concatenate([multipole, incoming.reshape(-1, 256)], axis=0)
-    whole = lax.all_gather(coarse_local, "gx", axis=0, tiled=True)
-    data = jnp.concatenate([positions, charges[None, :]], axis=0).reshape(4, 128, 128)
-    lower = shifted_2(data[:, 120:], ("gx", "gy"), 1)
-    upper = shifted_2(data[:, :8], ("gx", "gy"), -1)
-    ext = jnp.concatenate([lower, data, upper, jnp.zeros((4, 112, 128), F32)], axis=1)
-    leaf, pot = call(
-        table, whole, list_src, list_vec, list_len.reshape(4, 128), parent_of.reshape(4, 128), octant.reshape(4, 128),
-        near_list, ext, m2l_ops, l2l_ops, basis,
+        compiler_params=pltpu.CompilerParams(vmem_limit_bytes=63 << 20, collective_id=0, has_side_effects=True),
+    )(
+        multipole, coarse_local, send_rows[0].T, list_src.T, list_vec.T, list_len.reshape(4, 128), parent_of.reshape(4, 128),
+        octant.reshape(4, 128), near_list.T, positions, charges.reshape(128, 128), m2l_ops, l2l_ops,
+        basis.reshape(512, 2, 16, 256),
     )
     return leaf, pot.reshape(-1)
 

time: 83.2 us -> 55.4 us (0.67)
  starting transfers between devices: 21.1 us -> 0 us
  blocking collectives: 14.6 us -> 0 us
  Pallas kernels: 37.9 us -> 51.2 us
  matrix products: 2.87 us -> 0 us
  other arithmetic: 2.07 us -> 0 us
    all_gather x1 -> x0, blocking collectives: 14.6 us -> none  [shards(): whole = lax.all_gather(coarse_local, 'gx', axis=0, tiled=True)]
    pallas_call x1, Pallas kernels: 37.9 us -> 51.2 us  [shards(): pl.pallas_call(kernel, out_shape=(jax.ShapeDtypeStruct((512, 256), F32),...]
    all_to_all x1 -> x0, starting transfers between devices: 11.5 us -> none  [shards(): lax.all_to_all(outgoing, ('gx', 'gy'), split_axis=0, concat_axis=0, tiled...]
    ppermute x2 -> x0, starting transfers between devices: 9.64 us -> none  [shifted_2(): return lax.ppermute(shard, axis, pairs)]
    dot_general x1 -> x0, matrix products: 2.87 us -> none  [dot(): return jnp.dot(a, b, preferred_element_type=F32)]
    concatenate x2 -> x0, other arithmetic: 2.07 us -> none  [the longest x1 1.17 us: shards(): table = jnp.concatenate([multipole, incoming.reshape(-1, 256)], axis=0)]
    unnamed x19 -> x2, local copies, waits for them, and re-layouts: 3.36 us -> 3.34 us
  transfers between devices with their start and end apart: 3 -> 0, of which waited for: 0 -> 0; matrix products, arithmetic and copies ran while one was open for 4% -> 0% of each run, Pallas kernels for 0% -> 0%
where the time goes in v2:
time: 55.4 us; the launch traced here: 55.2 us
  Pallas kernels  51.2 us (92%)
  local copies, waits for them, and re-layouts  3.34 us (6%)
  between operations  0.64 us (1%)
    pallas_call x1, Pallas kernels, shards(): pl.pallas_call(kernel, out_shape=(jax.ShapeDtypeStruct((512, 256), F32),...  51.2 us
    unnamed x2, local copies, waits for them, and re-layouts  3.34 us

profile of v2, /device:TPU:1, one launch (start us, length us, event | category | flops | bytes accessed | tf_op | source)
XLA Modules:
  0.0 55.2 jit_solution(8088072441419129541)
XLA Ops:
  0.6 51.2 %shard_map.149 = (f32[512,256]{1,0:T(8,128)}, f32[128,128]{1,0:T(8,128)}) custom-call(bf16[512,256]{1,0:T(8,128)(2,1)} %multipole_ref.1, bf16[32,256]{1,0:T(8,128)(2,1)} %coarse_ref.1, s32[16,128]{1,0:T(8,128)} %bitcast.18, s32[64,512]{1,0:T(8,128)} %bitcast.13, s32[64,512]{1,0:T(8,128)} %bitcast.14, s32[4,128]{1,0:T(4,128)} %bitcast.19, s32[4,128]{1,0:T(4,128)} %bitcast.20, ...), custom_call_target="tpu_custom_call" | custom-call | tf_op jit(solution)/shard_map/pallas_call | solution.py:309
  51.8 1.9 %copy.18 = f32[512,256]{1,0:T(8,128)} copy(f32[512,256]{1,0:T(8,128)} %get-tuple-element.8) | data formatting | bytes 1048576
  53.7 1.5 %copy.19 = f32[16384]{0:T(1024)} copy(f32[16384]{0:T(1024)} %bitcast.16) | data formatting | bytes 131072

commit v3 on v2

--- a/solution.py
+++ b/solution.py
@@ -120,31 +120,41 @@
     return jnp.concatenate(parts, 0).T
 
 
-def group(i, n, own, incoming, S, G, Gb):
-    rows = 16 * n
-    lhs = [S[t, pl.ds(i * n, n)].reshape(rows, 256) for t in range(10)]
-    g = dot(jnp.concatenate(lhs[:2], 1), own[...]) + dot(jnp.concatenate(lhs[2:], 1), incoming[...].reshape(2048, 256))
-    G[0] = g[:, :128]
-    G[1] = g[:, 128:]
-    for v in range(16):
-        Gb[v, pl.ds(i * n, n), :] = jnp.concatenate(
-            [G[0, pl.ds(v, n, stride=16), :], G[1, pl.ds(v, n, stride=16), :]], 1
-        ).astype(BF)
-
-
-def coarse_rows(parent_ref, octant_ref, coarse, Gb):
+def group(i, n, first, count, rows_of, S, G, add):
+    rows = pl.ds(i * (16 * n), 16 * n)
+    lhs = [S[first + t, pl.ds(i * n, n)].reshape(16 * n, 256) for t in range(count)]
+    g = dot(jnp.concatenate(lhs, 1), rows_of)
+    for h in range(2):
+        part = g[:, 128 * h : 128 * h + 128]
+        G[h, rows, :] = G[h, rows, :] + part if add else part
+
+
+def coarse_rows(parent_ref, octant_ref, coarse, C, oct):
     for b in range(4):
+        rows = pl.ds(128 * b, 128)
         parent = column(parent_ref[pl.ds(b, 1), :].astype(F32))
-        octant = column(octant_ref[pl.ds(b, 1), :].astype(F32))
+        oct[rows, :] = column(octant_ref[pl.ds(b, 1), :].astype(F32))
         lane = iota((128, 128), 1).astype(F32)
         pick = jnp.concatenate([(parent == lane).astype(F32), (parent == lane + 128.0).astype(F32)], 1).astype(BF)
-        rows = dot(pick, coarse[...].reshape(256, 256))
-        octant = jnp.concatenate([octant, octant], 1)
-        for o in range(8):
-            Gb[16 + o, pl.ds(128 * b, 128), :] = jnp.where(octant == float(o), rows, 0.0).astype(BF)
-
-
-def far_rows(i, S, rounded, F):
+        C[rows, :] = dot(pick, coarse[...].reshape(256, 256))
+
+
+def leaves(h, n, G, C, oct, ops, leaf_ref, rounded):
+    rows = pl.ds(h * n, n)
+    parts = []
+    for v in range(16):
+        at = pl.ds(h * (16 * n) + v, n, stride=16)
+        parts.append(jnp.concatenate([G[0, at, :], G[1, at, :]], 1).astype(BF))
+    octant = jnp.concatenate([oct[rows, :]] * 2, 1)
+    coarse = C[rows, :]
+    for o in range(8):
+        parts.append(jnp.where(octant == float(o), coarse, 0.0).astype(BF))
+    leaf = dot(jnp.concatenate(parts, 1), ops[...].reshape(24 * 256, 256))
+    leaf_ref[rows, :] = leaf
+    rounded[rows, :] = leaf.astype(BF)
+
+
+def far_rows(i, S, rounded, near, pot_ref):
     pieces = []
     for c in range(16):
         pieces += [S[0, i * 16 + c], S[1, i * 16 + c]]
@@ -152,7 +162,8 @@
     r = jnp.where(iota((16, 512), 0) == (iota((16, 512), 1) >> 5), r, 0.0)
     r = jnp.sum(r, 0, keepdims=True)
     for h in range(4):
-        F[pl.ds(4 * i + h, 1), :] = r[:, 128 * h : 128 * h + 128]
+        row = pl.ds(4 * i + h, 1)
+        pot_ref[row, :] = near[row, :] + r[:, 128 * h : 128 * h + 128]
 
 
 def fill_data(pos_ref, charge_ref, E):
@@ -185,8 +196,8 @@
     multipole_ref, coarse_ref, send_ref, src_ref, vec_ref, len_ref, parent_ref, octant_ref, near_ref, pos_ref, charge_ref,
     m2l_hbm, l2l_hbm, basis_hbm,
     leaf_ref, pot_ref,
-    S, G, Gb, ops, rounded, hi0, hi1, lo, XT, Y, tgt, src, N, F, E, SG, outgoing, incoming, coarse,
-    sem_ops, sem_basis, send_sem, recv_sem, coarse_send, coarse_recv, rim_send, rim_recv,
+    S, G, ops, rounded, C, oct, hi0, hi1, lo, XT, Y, tgt, src, N, nearpot, E, SG, outgoing, incoming, coarse,
+    sem_ops, sem_basis, send_sem, recv_sem, coarse_send, coarse_recv, rim_send, rim_recv, entered,
 ):
     gx, gy = lax.axis_index("gx"), lax.axis_index("gy")
     me = gx * 16 + gy
@@ -195,11 +206,13 @@
 
     barrier = pltpu.get_barrier_semaphore()
 
-    def greet(o, _):
-        d = lax.rem(me + o, 128)
-        pl.semaphore_signal(barrier, inc=1, device_id=(d // 16, lax.rem(d, 16)), device_id_type=MESH)
-
-    lax.fori_loop(1, 128, greet, None)
+    def greet(sem, dx, dy):
+        pl.semaphore_signal(sem, inc=1, device_id=(lax.rem(gx + dx, 8), lax.rem(gy + dy, 16)), device_id_type=MESH)
+
+    for r in range(1, 8):
+        greet(barrier, r, 0)
+    for r in range(1, 16):
+        greet(barrier, 0, r)
     ops_in = [
         pltpu.make_async_copy(m2l_hbm, ops.at[pl.ds(0, 16)], sem_ops.at[0]),
         pltpu.make_async_copy(l2l_hbm, ops.at[pl.ds(16, 8)], sem_ops.at[1]),
@@ -207,8 +220,12 @@
     for c in ops_in:
         c.start()
     fill_data(pos_ref, charge_ref, E)
+    pl.semaphore_wait(barrier, 22)
+    for r in range(1, 8):
+        greet(entered, r, 0)
     pick_rows(send_ref, multipole_ref, SG, outgoing)
-    pl.semaphore_wait(barrier, 127)
+    codes(src_ref, vec_ref, len_ref, hi0, hi1, lo)
+    pl.semaphore_wait(entered, 7)
 
     def send(o):
         d = lax.rem(me + o, 128)
@@ -239,13 +256,19 @@
     def _():
         send_rim(False).start()
 
-    lax.fori_loop(1, 128, lambda o, _: send(o).start(), None)
-    lax.fori_loop(1, 8, lambda r, _: send_coarse(r).start(), None)
+    for o in range(1, 4):
+        send(o).start()
     incoming[me] = outgoing[me]
     coarse[gx] = coarse_ref[...]
 
-    codes(src_ref, vec_ref, len_ref, hi0, hi1, lo)
-    lax.fori_loop(0, 256, lambda p, _: count_pair(p, hi0, hi1, lo, S), None, unroll=32)
+    def count_and_send(i, _):
+        for u in range(32):
+            count_pair(i * 32 + u, hi0, hi1, lo, S)
+            if u < 31:
+                send(4 + i * 31 + u).start()
+
+    lax.fori_loop(0, 4, count_and_send, None)
+    lax.fori_loop(1, 8, lambda r, _: send_coarse(r).start(), None)
 
     @pl.when(me > 0)
     def _():
@@ -258,8 +281,17 @@
         send_rim(True).wait_send()
 
     near_prepare(E, near_ref, XT, Y, tgt, src)
-    for b in range(4):
-        lax.fori_loop(0, 8, lambda jj, _: near_unit(b, jj, 4, tgt, src, N), None)
+
+    def count_and_near(i, _):
+        for u in range(8):
+            for w in range(4):
+                count_pair(128 + i * 32 + 4 * u + w, hi0, hi1, lo, S)
+            near_unit(i, u, 4, tgt, src, N)
+
+    lax.fori_loop(0, 4, count_and_near, None)
+    nearpot[...] = near_rows(N)
+    blocks = 512 // NBLK
+    lax.fori_loop(0, blocks, lambda i, _: group(i, NBLK, 0, 2, multipole_ref[...], S, G, False), None)
 
     def all_of(ref, n, send_sem, recv_sem):
         part = ref.at[pl.ds(0, n)]
@@ -267,36 +299,29 @@
             src_ref=part, dst_ref=part, send_sem=send_sem, recv_sem=recv_sem, device_id=(gx, gy), device_id_type=MESH
         )
 
+    basis_in = [pltpu.make_async_copy(basis_hbm.at[:, h], S.at[h], sem_basis.at[h]) for h in range(2)]
+    for c in basis_in:
+        c.start()
     coarse_in = all_of(coarse, 7, coarse_send, coarse_recv)
     coarse_in.wait_send()
     coarse_in.wait_recv()
-    coarse_rows(parent_ref, octant_ref, coarse, Gb)
+    coarse_rows(parent_ref, octant_ref, coarse, C, oct)
     rows_in = all_of(incoming, 127, send_sem, recv_sem)
     rows_in.wait_send()
     rows_in.wait_recv()
-
-    def basis_copy(i, h):
-        cells = pl.ds(i * NBLK, NBLK)
-        return pltpu.make_async_copy(basis_hbm.at[cells, h], S.at[h, cells], sem_basis.at[i, h])
-
-    def block(i, _):
-        group(i, NBLK, multipole_ref, incoming, S, G, Gb)
-        basis_copy(i, 0).start()
-        basis_copy(i, 1).start()
-
-    lax.fori_loop(0, 512 // NBLK, block, None)
+    lax.fori_loop(0, blocks, lambda i, _: group(i, NBLK, 2, 8, incoming[...].reshape(2048, 256), S, G, True), None)
     for c in ops_in:
         c.wait()
     for h in range(2):
-        rows = pl.ds(256 * h, 256)
-        leaf = dot(jnp.concatenate([Gb[v, rows, :] for v in range(24)], 1), ops[...].reshape(24 * 256, 256))
-        leaf_ref[rows, :] = leaf
-        rounded[rows, :] = leaf.astype(BF)
-    for i in range(512 // NBLK):
-        basis_copy(i, 0).wait()
-        basis_copy(i, 1).wait()
-    lax.fori_loop(0, 32, lambda i, _: far_rows(i, S, rounded, F), None, unroll=4)
-    pot_ref[...] = F[...] + near_rows(N)
+        leaves(h, 256, G, C, oct, ops, leaf_ref, rounded)
+    for c in basis_in:
+        c.wait()
+    lax.fori_loop(0, 32, lambda i, _: far_rows(i, S, rounded, nearpot, pot_ref), None, unroll=4)
+
+
+def results(leaf_in, pot_in, leaf_out, pot_out):
+    leaf_out[...] = leaf_in[...]
+    pot_out[...] = pot_in[...]
 
 
 def shards(
@@ -306,17 +331,19 @@
     vmem = pl.BlockSpec(memory_space=pltpu.VMEM)
     hbm = pl.BlockSpec(memory_space=pl.ANY)
     dma = pltpu.SemaphoreType.DMA
+    outs = (jax.ShapeDtypeStruct((512, 256), F32), jax.ShapeDtypeStruct((128, 128), F32))
     leaf, pot = pl.pallas_call(
         kernel,
-        out_shape=(jax.ShapeDtypeStruct((512, 256), F32), jax.ShapeDtypeStruct((128, 128), F32)),
+        out_shape=outs,
         in_specs=[vmem] * 11 + [hbm] * 3,
         out_specs=(vmem, vmem),
         scratch_shapes=[
             pltpu.VMEM((10, 512, 16, 256), BF),
-            pltpu.VMEM((2, 16 * NBLK, 128), F32),
-            pltpu.VMEM((24, 512, 256), BF),
+            pltpu.VMEM((2, 8192, 128), F32),
             pltpu.VMEM((24, 256, 256), BF),
             pltpu.VMEM((512, 256), BF),
+            pltpu.VMEM((512, 256), F32),
+            pltpu.VMEM((512, 128), F32),
             pltpu.VMEM((256, 128), F32),
             pltpu.VMEM((256, 128), F32),
             pltpu.VMEM((256, 128), F32),
@@ -331,7 +358,7 @@
             pltpu.VMEM((128, 16, 256), BF),
             pltpu.VMEM((128, 16, 256), BF),
             pltpu.VMEM((8, 32, 256), BF),
-            dma((2,)), dma((512 // NBLK, 2)), dma, dma, dma, dma, dma((2,)), dma((2,)),
+            dma((2,)), dma((2,)), dma, dma, dma, dma, dma((2,)), dma((2,)), pltpu.SemaphoreType.REGULAR,
         ],
         compiler_params=pltpu.CompilerParams(vmem_limit_bytes=63 << 20, collective_id=0, has_side_effects=True),
     )(
@@ -339,6 +366,9 @@
         octant.reshape(4, 128), near_list.T, positions, charges.reshape(128, 128), m2l_ops, l2l_ops,
         basis.reshape(512, 2, 16, 256),
     )
+    leaf, pot = pl.pallas_call(
+        results, out_shape=outs, in_specs=[vmem] * 2, out_specs=(vmem, vmem)
+    )(leaf, pot)
     return leaf, pot.reshape(-1)
 
 

time: 55.4 us -> 71.8 us (1.30)
  Pallas kernels: 51.2 us -> 71 us
  local copies, waits for them, and re-layouts: 3.34 us -> 0 us
    pallas_call x1 -> x2, Pallas kernels: 51.2 us -> 71 us  [the longest x1 69.1 us: shards(): pl.pallas_call(kernel, out_shape=outs, in_specs=[vmem] * 11 + [hbm] * 3,...]
    unnamed x2 -> x0, local copies, waits for them, and re-layouts: 3.34 us -> none
where the time goes in v3:
time: 71.8 us; the launch traced here: 71.6 us
  Pallas kernels  71 us (99%)
    pallas_call x1, Pallas kernels, shards(): pl.pallas_call(kernel, out_shape=outs, in_specs=[vmem] * 11 + [hbm] * 3,...  69.1 us
    pallas_call x1, Pallas kernels, shards(): pl.pallas_call(results, out_shape=outs, in_specs=[vmem] * 2, out_specs=(v...  1.88 us

profile of v3, /device:TPU:1, one launch (start us, length us, event | category | flops | bytes accessed | tf_op | source)
XLA Modules:
  0.0 71.6 jit_solution(17254793678168462819)
XLA Ops:
  0.6 69.1 %shard_map.149 = (f32[512,256]{1,0:T(8,128)}, f32[128,128]{1,0:T(8,128)}) custom-call(bf16[512,256]{1,0:T(8,128)(2,1)} %multipole_ref.1, bf16[32,256]{1,0:T(8,128)(2,1)} %coarse_ref.1, s32[16,128]{1,0:T(8,128)} %bitcast.17, s32[64,512]{1,0:T(8,128)} %bitcast.13, s32[64,512]{1,0:T(8,128)} %bitcast.14, s32[4,128]{1,0:T(4,128)} %bitcast.18, s32[4,128]{1,0:T(4,128)} %bitcast.19, ...), custom_call_target="tpu_custom_call" | custom-call | tf_op jit(solution)/shard_map/pallas_call | solution.py:335
  69.7 1.9 %shard_map.150 = (f32[512,256]{1,0:T(8,128)}, f32[128,128]{1,0:T(8,128)}) custom-call(f32[512,256]{1,0:T(8,128)} %get-tuple-element.6.leaf_in, f32[128,128]{1,0:T(8,128)} %get-tuple-element.7.pot_in), custom_call_target="tpu_custom_call" | custom-call | tf_op jit(solution)/shard_map/pallas_call | solution.py:369
